TPU v7x, 32 devices: a whole 2x2x4 slice. The times are simulated.
32 devices in a mesh: row: 4 (over y, core), col: 8 (over z, x).
Axes of the slice: x: 2, y: 2, z: 4, core: 2. Of those that a mesh axis runs over, the one named last changes fastest.
Arguments:
- a_vals: bfloat16 [256, 131072], P('row', 'col'), may hold values from -1.1953125 to 1.1953125
- p_vals: bfloat16 [64, 16384], P(None, ('row', 'col')), may hold values from -0.75 to 0.75
- a_rows: int32 [4, 2048], P('row', 'col'), may hold values from 0 to 63, as said below
- a_cols: int32 [4, 2048], P('row', 'col'), may hold values from 0 to 31, as said below
- a_count: int32 [4, 8], P('row', 'col'), may hold values from 64 to 256, as said below
- c_slot: int32 [4, 2048], P('row', 'col'), may hold values from 0 to 5, as said below
- agg: int32 [256], P(('row', 'col')), may hold values from 0 to 7, as said below
Outputs:
- coarse_vals: float32 [32, 24576], P(('row', 'col'))
Inputs may be any that keep to these rules, and one draw needn't show every extreme that they name: Each tile's live slots are its first a_count ones; some tile of every row group has all 256 slots live. `agg`: in each row group, the aggregate numbers t*32//8 to (t+1)*32//8 - 1 are taken by the fine block rows of the row group's t-th column group of 32 rows, each number by exactly 8 of them. Coarse pattern: in row group r, slot k of coarse row a belongs to column group (a*6 + k + o_r) mod 8, for one shift o_r of the row group, and to one aggregate of that column group; every tile slot, live or not, has a fine row of aggregate a and a fine column of that slot's aggregate, with c_slot = k. The live slots of each tile reach every (a, k) pair of its column group. `a_rows`: see c_slot. `a_cols`: see c_slot.
All inputs are finite; a program needn't handle non-finite values.
Results may differ from a plain program's by a relative error of at most 0.0049.
Values may be sent and summed in bfloat16 or wider, within the bound.
A program may use at most 64 MiB of HBM per device.

v0:
```python
import jax
import jax.numpy as jnp
from jax import lax
from jax.sharding import PartitionSpec as P

AGG = 8
KC = 6


def from_root(x, axis, root):
    mine = lax.axis_index(axis) == root
    return lax.psum(jnp.where(mine, x, jnp.zeros_like(x)), axis)


def on_device(a_vals, p_vals, a_rows, a_cols, a_count, c_slot, agg):
    block_width = p_vals.shape[0]
    block_area = block_width * block_width
    col_total = lax.axis_size("col")
    row_total = lax.axis_size("row")
    col_ratio = col_total // row_total
    row_panel, row_agg = (
        lax.all_gather(p_vals, "col", axis=1, tiled=True),
        lax.all_gather(agg, "col", axis=0, tiled=True),
    )
    rows_group = row_agg.shape[0]
    cols_group = rows_group // col_ratio
    col_index = lax.axis_index("col")
    offset = col_index % col_ratio * cols_group * block_width
    own_slice = lax.dynamic_slice_in_dim(row_panel, offset, cols_group * block_width, 1)
    col_panel = from_root(own_slice, "row", col_index // col_ratio)
    row_blocks = row_panel.reshape(block_width, rows_group, block_width)
    col_blocks = col_panel.reshape(block_width, cols_group, block_width)
    slot_total = a_rows.shape[1]
    tile_blocks = a_vals.reshape(block_width, slot_total, block_width)
    slot_rows = a_rows[0]
    slot_cols = a_cols[0]
    coarse_slot = c_slot[0]
    live_count = a_count[0, 0]
    coarse_rows = rows_group // AGG
    segments = coarse_rows * KC
    segment_ids = jnp.arange(segments, dtype=jnp.int32)
    left = jnp.take(row_blocks, slot_rows, axis=1)
    half = jnp.einsum("fsa,fsj->saj", left, tile_blocks, preferred_element_type=jnp.float32).astype(
        jnp.bfloat16
    )
    right = jnp.take(col_blocks, slot_cols, axis=1)
    triple = jnp.einsum("saj,jsb->sab", half, right, preferred_element_type=jnp.float32).astype(
        jnp.bfloat16
    )
    live_mask = jnp.arange(slot_total, dtype=jnp.int32) < live_count
    target = jnp.take(row_agg, slot_rows) * KC + coarse_slot
    selector = ((target[None, :] == segment_ids[:, None]) & live_mask[None, :]).astype(jnp.bfloat16)
    partial_value = jnp.dot(
        selector, triple.reshape(slot_total, block_area), preferred_element_type=jnp.float32
    )
    owner_rows = coarse_rows // col_total
    width = owner_rows * KC
    capacity = (width + col_total - 1) // col_total
    live_all = jnp.arange(slot_total, dtype=jnp.int32) < live_count
    all_target = jnp.take(row_agg, slot_rows) * KC + coarse_slot
    present = jnp.any(
        (all_target[None, :] == segment_ids[:, None]) & live_all[None, :], axis=1
    ).reshape(col_total, width)
    rank = jnp.cumsum(present.astype(jnp.int32), axis=1) - 1
    picked = present[:, None, :] & (
        rank[:, None, :] == jnp.arange(capacity, dtype=jnp.int32)[None, :, None]
    )
    terms = partial_value.astype(jnp.bfloat16).reshape(col_total, width, block_area)
    send_vals = jnp.einsum(
        "oce,oed->ocd", picked.astype(jnp.bfloat16), terms, preferred_element_type=jnp.float32
    ).astype(jnp.bfloat16)
    positions = jnp.arange(width, dtype=jnp.float32)
    send_ids = jnp.where(
        jnp.any(picked, axis=2),
        jnp.sum(picked.astype(jnp.float32) * positions[None, None, :], axis=2),
        float(width),
    ).astype(jnp.bfloat16)
    got_vals, got_ids = (
        lax.all_to_all(send_vals, "col", split_axis=0, concat_axis=0, tiled=True),
        lax.all_to_all(send_ids, "col", split_axis=0, concat_axis=0, tiled=True),
    )
    placing = (
        got_ids.reshape(col_total * capacity)[:, None] == positions.astype(jnp.bfloat16)[None, :]
    ).astype(jnp.bfloat16)
    dense = jnp.dot(
        placing.T,
        got_vals.reshape(col_total * capacity, block_area),
        preferred_element_type=jnp.float32,
    )
    return dense.reshape(owner_rows, KC * block_area)


def solution(mesh):
    return jax.shard_map(
        on_device,
        mesh=mesh,
        in_specs=(
            P("row", "col"),
            P(None, ("row", "col")),
            P("row", "col"),
            P("row", "col"),
            P("row", "col"),
            P("row", "col"),
            P(("row", "col")),
        ),
        out_specs=P(("row", "col"), None),
        check_vma=False,
    )
```

profile of v0, /device:TPU:0, one launch (start us, length us, event | category | flops | bytes accessed | tf_op | source)
XLA Modules:
  0.0 120.8 jit_solution(12556651776064868247)
XLA Ops:
  6.5 33.4 %all_gather.7 = bf16[64,4096]{1,0:T(8,128)(2,1)S(1)} all-gather(bf16[64,512]{1,0:T(8,128)(2,1)} %param.10), channel_id=1, replica_groups=mesh['row'=4,'col'=8] {'col'}, dimensions={1}, use_global_device_ids=true | all-gather | bytes 589824 | tf_op jit(solution)/shard_map/all_gather | solution.py:22
  40.5 1.1 copy.31
  41.6 1.2 %dynamic-slice = u32[1]{0:T(128)} dynamic-slice(u32[32]{0:T(128)} %constant.102, u32[]{:T(128)S(6)} %add.87), dynamic_slice_sizes={1} | dynamic-slice | bytes 12
  43.5 0.9 dynamic-update-slice
  44.3 10.9 %all-reduce = s32[64]{0:T(128)S(1)} all-reduce(s32[64]{0:T(128)S(1)} %dynamic-update-slice), channel_id=1, replica_groups=mesh['row'=4,'col'=8] {'col'}, use_global_device_ids=true, to_apply=%add | all-reduce | flops 64 | bytes 512
  55.3 0.7 compare_select_fusion.2
  56.6 1.9 %gather_fusion.2 = s32[256]{0:T(256)S(1)} fusion(s32[64]{0:T(128)S(1)} %all-reduce, s32[1024]{0:T(1024)S(1)} %pad_clamp_fusion.2), kind=kCustom, calls=%fused_computation.clone | custom fusion | bytes 3072 | tf_op jit(solution)/shard_map/jit(_take)/gather | solution.py:60
  59.2 0.7 copy.27
  59.9 3.3 %all-to-all-start = ((bf16[8,1,1]{2,1,0:T(2,128)(2,1)}), bf16[8,1,1]{2,1,0:T(2,128)(2,1)S(1)}, u32[]{:S(2)}, u32[]{:S(2)}) async-start(bf16[8,1,1]{2,1,0:T(2,128)(2,1)} %copy.27), calls=%async_computation | async-start | bytes 8192 | tf_op jit(solution)/shard_map/all_to_all | solution.py:80
  63.3 1.1 reshape.185
  64.4 0.7 copy.28
  65.1 6.5 %reshape.186 = bf16[64,256,64]{2,1,0:T(8,128)(2,1)} reshape(bf16[64,16384]{1,0:T(8,128)(2,1)} %param.9) | data formatting | bytes 4194304 | tf_op jit(solution)/shard_map/reshape | solution.py:34
  71.6 3.1 %gather_fusion = bf16[256,64,64]{2,1,0:T(8,128)(2,1)} fusion(bf16[64,64,64]{2,0,1:T(8,128)(2,1)S(1)} %copy.28, s32[1024]{0:T(1024)S(1)} %pad_clamp_fusion.1), kind=kCustom, calls=%fused_computation.1 | custom fusion | bytes 4195328 | tf_op jit(solution)/shard_map/jit(_take)/gather | solution.py:42
  74.7 1.5 %all-reduce.3.cloned.1.call-done = bf16[64,32,64]{2,0,1:T(8,128)(2,1)} async-done(((bf16[64,32,64]{2,0,1:T(8,128)(2,1)}), bf16[64,32,64]{2,0,1:T(8,128)(2,1)}) %all-reduce.3.cloned.1.call-update) | async-done | bytes 262160 | tf_op jit(solution)/shard_map/psum | solution.py:12
  76.2 4.1 %gather_fusion.1 = bf16[256,64,64]{2,1,0:T(8,128)(2,1)} fusion(bf16[64,32,64]{2,0,1:T(8,128)(2,1)} %all-reduce.3.cloned.1.call-done, s32[1024]{0:T(1024)S(1)} %pad_clamp_fusion), kind=kCustom, calls=%fused_computation.2 | custom fusion | bytes 4195328 | tf_op jit(solution)/shard_map/jit(_take)/gather | solution.py:46
  80.3 12.1 %fusion.10 = bf16[256,64,64]{2,1,0:T(8,128)(2,1)} fusion(bf16[256,64,64]{2,1,0:T(8,128)(2,1)} %gather_fusion.1, pred[256]{0:T(512)(128)(4,1)S(1)} %compare_and_fusion.1, bf16[64,256,64]{2,1,0:T(8,128)(2,1)} %reshape.186, bf16[256,64,64]{2,1,0:T(8,128)(2,1)} %gather_fusion, pred[256]{0:T(512)(128)(4,1)S(1)} %get-tuple-element.9), kind=kOutput, calls=%fused_computation.15 | convolution fusion | flops 272629760 | bytes 8389120 | tf_op jit(solution)/shard_map/saj,jsb->sab/dot_general | solution.py:47
  92.4 4.9 %copy.32 = bf16[256,64,64]{0,2,1:T(8,128)(2,1)S(1)} copy(bf16[256,64,64]{2,1,0:T(8,128)(2,1)} %fusion.10) | data formatting | bytes 4194304 | tf_op jit(solution)/shard_map/convert_element_type | solution.py:47
  97.3 0.7 convolution_convert_fusion
  98.6 0.5 broadcast.165
  99.1 0.7 reduce.3
  99.8 0.7 reshape.227
  100.4 5.5 %all-to-all-start.1 = ((bf16[8,2,2048]{2,1,0:T(2,128)(2,1)}), bf16[8,2,2048]{2,1,0:T(2,128)(2,1)S(1)}, u32[]{:S(2)}, u32[]{:S(2)}) async-start(bf16[8,2,2048]{2,1,0:T(2,128)(2,1)} %reshape.227), calls=%async_computation.1 | async-start | bytes 131072 | tf_op jit(solution)/shard_map/all_to_all | solution.py:79
  106.1 6.7 %all-to-all-done.1 = bf16[8,2,2048]{2,1,0:T(2,128)(2,1)S(1)} async-done(((bf16[8,2,2048]{2,1,0:T(2,128)(2,1)}), bf16[8,2,2048]{2,1,0:T(2,128)(2,1)S(1)}, u32[]{:S(2)}, u32[]{:S(2)}) %all-to-all-start.1) | async-done | bytes 65568 | tf_op jit(solution)/shard_map/all_to_all | solution.py:79
  113.2 0.7 copy.38
  (36 shorter events, 2.3 us)
Async XLA Ops:
  6.5 52.0 %copy-start = (s32[1,256]{1,0:T(1,128)S(1)}, s32[1,256]{1,0:T(1,128)}, u32[]{:S(2)}) copy-start(s32[1,256]{1,0:T(1,128)} %param.11) | copy-start | bytes 3076
  6.5 52.0 %copy-start.2 = (s32[1,256]{1,0:T(1,128)S(1)}, s32[1,256]{1,0:T(1,128)}, u32[]{:S(2)}) copy-start(s32[1,256]{1,0:T(1,128)} %param.14) | copy-start | bytes 3076
  6.5 56.7 %copy-start.1 = (s32[1,256]{1,0:T(1,128)S(1)}, s32[1,256]{1,0:T(1,128)}, u32[]{:S(2)}) copy-start(s32[1,256]{1,0:T(1,128)} %param.12) | copy-start | bytes 3076
  6.5 69.7 %all-reduce.3.cloned.1.call-start = ((), (), s32[]{:S(2)}) async-start(), calls=%async_computation.2 | async-start | bytes 1048576 | tf_op jit(solution)/shard_map/psum | solution.py:12
  59.9 40.5 %all-to-all-start = ((bf16[8,1,1]{2,1,0:T(2,128)(2,1)}), bf16[8,1,1]{2,1,0:T(2,128)(2,1)S(1)}, u32[]{:S(2)}, u32[]{:S(2)}) async-start(bf16[8,1,1]{2,1,0:T(2,128)(2,1)} %copy.27), calls=%async_computation | async-start | bytes 8192 | tf_op jit(solution)/shard_map/all_to_all | solution.py:80
  100.4 12.4 %all-to-all-start.1 = ((bf16[8,2,2048]{2,1,0:T(2,128)(2,1)}), bf16[8,2,2048]{2,1,0:T(2,128)(2,1)S(1)}, u32[]{:S(2)}, u32[]{:S(2)}) async-start(bf16[8,2,2048]{2,1,0:T(2,128)(2,1)} %reshape.227), calls=%async_computation.1 | async-start | bytes 131072 | tf_op jit(solution)/shard_map/all_to_all | solution.py:79
Sparse Core Ops, SparseCore 0:
  41.7 34.4 all-reduce.2
where the time goes:
time: 121 us
  blocking collectives  44.3 us (37%)
  local copies, waits for them, and re-layouts  29 us (24%)
  between operations  14.9 us (12%)
  matrix products  13.4 us (11%)
  starting transfers between devices  8.8 us (7%)
  waiting for transfers between devices  8.3 us (7%)
  other arithmetic  2.13 us (2%)
    all_gather x1, blocking collectives, on_device(): lax.all_gather(p_vals, 'col', axis=1, tiled=True)  33.4 us
    dot_general x1, matrix products, on_device(): jnp.einsum('saj,jsb->sab', half, right, preferred_element_type=jnp.float32)  12.1 us
    unnamed x1, blocking collectives  10.9 us
    all_to_all x1, waiting for transfers between devices, on_device(): lax.all_to_all(send_vals, 'col', split_axis=0, concat_axis=0, tiled=True)  6.75 us
    reshape x1, local copies, waits for them, and re-layouts, on_device(): tile_blocks = a_vals.reshape(block_width, slot_total, block_width)  6.48 us
    all_to_all x1, starting transfers between devices, on_device(): lax.all_to_all(send_vals, 'col', split_axis=0, concat_axis=0, tiled=True)  5.51 us
    convert_element_type x1, local copies, waits for them, and re-layouts, on_device(): jnp.einsum('saj,jsb->sab', half, right, preferred_element_type=jnp.float32)  4.92 us
    gather x1, local copies, waits for them, and re-layouts, on_device(): right = jnp.take(col_blocks, slot_cols, axis=1)  4.11 us
  transfers between devices with their start and end apart: 3, of which 2 were waited for; matrix products, arithmetic and copies ran while one was open for 35% of the time, Pallas kernels for 0%

commit v1 on v0

v1 whole, which is shorter than its diff:
```python
import functools

import jax
import jax.numpy as jnp
from jax import lax
from jax.experimental import pallas as pl
from jax.experimental.pallas import tpu as pltpu
from jax.sharding import PartitionSpec as P

AGG = 8
KC = 6
LO = 2
UNROLL = 8
MESH = pl.DeviceIdType.MESH
F32 = jnp.float32
BF16 = jnp.bfloat16


def kernel(
    n_row, n_col, pk_ref, idx_ref, k0_ref, a_hbm, p_ref, ag_ref, out_ref,
    a_v, pan, agp, colp, pz, ps, q_ref, snd, rcv,
    a_sem, p_send, p_recv, g_send, g_recv, c_send, c_recv, x_send, x_recv,
):
    bw = p_ref.shape[0]
    dev_rows = ag_ref.shape[0]
    slots = ps.shape[0] - 1
    ratio = n_col // n_row
    per = n_col // ratio
    owners = per * dev_rows // AGG
    hi = n_col // LO
    row = lax.axis_index("row")
    me = lax.axis_index("col")
    z, x = me // LO, lax.rem(me, LO)
    is_root = row == me // ratio
    part = lax.rem(me, ratio)

    @pl.loop(0, slots // 2)
    def _(i):
        lanes = pl.ds(pl.multiple_of(i * (2 * bw), 2 * bw), 2 * bw)
        pltpu.make_async_copy(a_hbm.at[:, lanes], a_v.at[i], a_sem).start()

    def col_of(d):
        return lax.rem(me + d, n_col)

    barrier = pltpu.get_barrier_semaphore()
    for d in range(1, n_col):
        pl.semaphore_signal(barrier, inc=1, device_id=(row, col_of(d)), device_id_type=MESH)
    for d in range(1, n_row):
        pl.semaphore_signal(
            barrier, inc=1, device_id=(lax.rem(row + d, n_row), me), device_id_type=MESH
        )
    pan[me] = p_ref[...]
    agp[me] = ag_ref[...]
    pl.semaphore_wait(barrier, n_col + n_row - 2)

    def remote(src, dst, s, r, dev):
        return pltpu.make_async_remote_copy(
            src_ref=src, dst_ref=dst, send_sem=s, recv_sem=r, device_id=dev, device_id_type=MESH
        )

    own = []
    for d in range(1, hi):
        to = lax.rem(z + d, hi) * LO + x
        own.append(remote(p_ref, pan.at[me], p_send.at[len(own)], p_recv.at[me], (row, to)))
    partner = z * LO + (1 - x)
    own.append(remote(p_ref, pan.at[me], p_send.at[len(own)], p_recv.at[me], (row, partner)))
    for c in own:
        c.start()

    def panel_copies(q, src):
        m = lax.rem(q, per)
        return [
            remote(
                src, colp.at[m], c_send.at[m, d - 1], c_recv.at[m],
                (lax.rem(row + d, n_row), me),
            )
            for d in range(1, n_row)
        ]

    def hand_on(q, src):
        @pl.when(is_root & (q // per == part))
        def _():
            for c in panel_copies(q, src):
                c.start()

    hand_on(me, p_ref)
    marks = [
        remote(ag_ref, agp.at[me], g_send.at[d - 1], g_recv.at[me], (row, col_of(d)))
        for d in range(1, n_col)
    ]
    for c in marks:
        c.start()

    pz[...] = jnp.zeros_like(pz)
    ps[slots] = jnp.zeros((bw, bw), BF16)
    q_ref[...] = jnp.zeros_like(q_ref)

    def landed(q):
        remote(p_ref, pan.at[q], p_send.at[0], p_recv.at[q], (row, partner)).wait_recv()

    passed = []
    landed(partner)
    hand_on(partner, pan.at[partner])
    for d in range(1, hi):
        q = lax.rem(z + hi - d, hi) * LO + x
        landed(q)
        c = remote(
            pan.at[q], pan.at[q], p_send.at[hi - 1 + d], p_recv.at[q], (row, partner)
        )
        c.start()
        passed.append(c)
        hand_on(q, pan.at[q])
    for d in range(1, hi):
        q = lax.rem(z + hi - d, hi) * LO + (1 - x)
        landed(q)
        hand_on(q, pan.at[q])

    for m in range(per):
        @pl.when(is_root)
        def _():
            colp[m] = pan[part * per + m]

        @pl.when(jnp.logical_not(is_root))
        def _():
            remote(
                p_ref, colp.at[m], c_send.at[m, 0], c_recv.at[m], (row, partner)
            ).wait_recv()

        for b in range(dev_rows):
            block = colp[m, :, b * bw:(b + 1) * bw]
            pz[2 * (m * dev_rows + b), 0:bw, :] = block
            pz[2 * (m * dev_rows + b) + 1, bw:2 * bw, :] = block
    pltpu.make_async_copy(a_v, a_v, a_sem).wait()

    def steps(it, acc):
        for u in range(UNROLL):
            at = it * UNROLL + u
            left = a_v[pk_ref[0, at]]
            right = pz[pk_ref[1, at]]
            keep = pk_ref[2, at].astype(F32)
            prod = jnp.dot(left, right, preferred_element_type=F32)
            acc = acc * keep + prod
            ps[at] = acc.astype(BF16)
        return acc

    lax.fori_loop(0, slots // UNROLL, steps, jnp.zeros((bw, bw), F32))

    for d in range(1, n_col):
        q = col_of(d)
        remote(ag_ref, agp.at[q], g_send.at[0], g_recv.at[q], (row, partner)).wait_recv()

    lane = lax.broadcasted_iota(jnp.int32, (1, 2 * bw), 1)

    def fold(c, carry):
        group = c // per
        base = (group * owners).astype(F32)
        total = jnp.zeros((owners * bw, bw), F32)
        for h in range(dev_rows // 4):
            wide = []
            for e in range(2):
                b = 4 * h + 2 * e
                flip = pan[c, :, b * bw:(b + 2) * bw].T
                pair = jnp.concatenate([flip[:bw], flip[bw:]], axis=1)
                mark = jnp.where(lane < bw, agp[c, b:b + 1, :], agp[c, b + 1:b + 2, :]) - base
                wide.append(
                    jnp.concatenate(
                        [pair * jnp.where(mark == o, 1.0, 0.0).astype(BF16) for o in range(owners)],
                        axis=0,
                    )
                )
            right = jnp.concatenate(
                [ps[idx_ref[0, c * dev_rows + 4 * h + e]] for e in range(4)], axis=0
            )
            total += jnp.dot(
                jnp.concatenate(wide, axis=1), right, preferred_element_type=F32
            )
        q_ref[group] += total
        return carry

    lax.fori_loop(0, n_col, fold, 0)

    half = bw // 2
    for o in range(n_col):
        g, w = o // owners, o % owners
        even = q_ref[g, pl.ds(w * bw, half, stride=2), :]
        odd = q_ref[g, pl.ds(w * bw + 1, half, stride=2), :]
        snd[o] = jnp.concatenate([even, odd], axis=1).astype(BF16)
    terms = []
    for d in range(1, n_col):
        to = col_of(d)
        terms.append(remote(snd.at[to], rcv.at[me], x_send.at[d - 1], x_recv.at[me], (row, to)))
    for c in terms:
        c.start()
    rcv[me] = snd[me]

    there = lax.broadcasted_iota(jnp.int32, (dev_rows, 2 * bw), 0) == k0_ref[0, 1]
    spot = jnp.sum(jnp.where(there, agp[k0_ref[0, 0]], 0.0), axis=0, keepdims=True)
    spot = spot.astype(jnp.int32) * KC + k0_ref[0, 2]
    for d in range(1, n_col):
        q = col_of(d)
        remote(snd.at[0], rcv.at[q], x_send.at[0], x_recv.at[q], (row, partner)).wait_recv()
    sums = [jnp.zeros((half, 2 * bw), F32) for _ in range(KC)]
    for c in range(n_col):
        value = rcv[c].astype(F32)
        where = (spot + (c - (KC + 1) * me + 8 * n_col * n_col)) & (n_col - 1)
        for k in range(KC):
            sums[k] += jnp.where(where == k, value, 0.0)
    for k in range(KC):
        out_ref[k * half:(k + 1) * half, :] = sums[k]

    for c in own + passed + marks + terms:
        c.wait_send()
    for m in range(per):
        @pl.when(is_root)
        def _():
            for c in panel_copies(m, pan.at[0]):
                c.wait_send()


def on_device(n_row, n_col, a_vals, p_vals, a_rows, a_cols, a_count, c_slot, agg):
    bw = p_vals.shape[0]
    dev_rows = agg.shape[0]
    slots = a_rows.shape[1]
    rows_group = dev_rows * n_col
    ratio = n_col // n_row
    cols_group = rows_group // ratio
    per = n_col // ratio
    assert rows_group // AGG == n_col and n_col & (n_col - 1) == 0 and n_col >= KC
    cb = (cols_group - 1).bit_length()
    sb = (slots - 1).bit_length()
    ids = jnp.arange(slots, dtype=jnp.int32)
    key = jnp.where(ids < a_count[0, 0], a_rows[0], rows_group)
    word = (((key << sb) | ids) << cb) | a_cols[0]
    rank = jnp.sum((word[None, :] < word[:, None]).astype(jnp.int32), axis=1)
    packed = jnp.sum(jnp.where(rank[None, :] == ids[:, None], word[None, :], 0), axis=1)
    tops = packed >> (cb + sb)
    keep = jnp.concatenate([jnp.zeros((1,), jnp.int32), (tops[1:] == tops[:-1]).astype(jnp.int32)])
    slot = (packed >> cb) & ((1 << sb) - 1)
    col = packed & ((1 << cb) - 1)
    plan = jnp.stack([slot >> 1, 2 * col + (slot & 1), keep])
    rows = jnp.arange(rows_group, dtype=jnp.int32)
    upto = jnp.sum((key[None, :] <= rows[:, None]).astype(jnp.int32), axis=1)
    seen = jnp.any(key[None, :] == rows[:, None], axis=1)
    last = jnp.where(seen, upto - 1, slots)
    lead = jnp.stack([a_rows[0, 0] // dev_rows, a_rows[0, 0] % dev_rows, c_slot[0, 0]])[None]
    marks = jnp.broadcast_to(agg.astype(F32)[:, None], (dev_rows, 2 * bw))
    smem = pl.BlockSpec(memory_space=pltpu.SMEM)
    vmem = pl.BlockSpec(memory_space=pltpu.VMEM)
    dma = pltpu.SemaphoreType.DMA
    owners = per * dev_rows // AGG
    out = pl.pallas_call(
        functools.partial(kernel, n_row, n_col),
        out_shape=jax.ShapeDtypeStruct((KC * bw // 2, 2 * bw), F32),
        in_specs=[smem, smem, smem, pl.BlockSpec(memory_space=pl.ANY), vmem, vmem],
        out_specs=vmem,
        scratch_shapes=[
            pltpu.VMEM((slots // 2, bw, 2 * bw), BF16),
            pltpu.VMEM((n_col, bw, dev_rows * bw), BF16),
            pltpu.VMEM((n_col, dev_rows, 2 * bw), F32),
            pltpu.VMEM((per, bw, dev_rows * bw), BF16),
            pltpu.VMEM((2 * cols_group, 2 * bw, bw), BF16),
            pltpu.VMEM((slots + 1, bw, bw), BF16),
            pltpu.VMEM((ratio, owners * bw, bw), F32),
            pltpu.VMEM((n_col, bw // 2, 2 * bw), BF16),
            pltpu.VMEM((n_col, bw // 2, 2 * bw), BF16),
            dma,
            dma((n_col,)), dma((n_col,)),
            dma((n_col,)), dma((n_col,)),
            dma((per, n_row)), dma((per,)),
            dma((n_col,)), dma((n_col,)),
        ],
        compiler_params=pltpu.CompilerParams(
            collective_id=0, has_side_effects=True, vmem_limit_bytes=48 << 20
        ),
    )(plan, last.reshape(1, rows_group), lead, a_vals, p_vals, marks)
    return out.reshape(1, KC * bw * bw)


def solution(mesh):
    return jax.shard_map(
        functools.partial(on_device, mesh.shape["row"], mesh.shape["col"]),
        mesh=mesh,
        in_specs=(
            P("row", "col"),
            P(None, ("row", "col")),
            P("row", "col"),
            P("row", "col"),
            P("row", "col"),
            P("row", "col"),
            P(("row", "col")),
        ),
        out_specs=P(("row", "col"), None),
        check_vma=False,
    )
```

time: 121 us -> 47.8 us (0.40)
  blocking collectives: 44.3 us -> 0 us
  Pallas kernels: 0 us -> 35.6 us
  local copies, waits for them, and re-layouts: 29 us -> 5.46 us
  matrix products: 13.4 us -> 0 us
  between operations: 14.9 us -> 2.96 us
  starting transfers between devices: 8.8 us -> 0 us
  waiting for transfers between devices: 8.3 us -> 0 us
  other arithmetic: 2.13 us -> 3.4 us
    pallas_call x0 -> x1, Pallas kernels: none -> 35.6 us  [on_device(): pl.pallas_call(functools.partial(kernel, n_row, n_col), out_shape=jax.Sha...]
    all_gather x1 -> x0, blocking collectives: 33.4 us -> none  [on_device(): lax.all_gather(p_vals, 'col', axis=1, tiled=True)]
    dot_general x4 -> x0, matrix products: 13.4 us -> none  [the longest x1 12.1 us: on_device(): jnp.einsum('saj,jsb->sab', half, right, preferred_element_type=jnp.float32)]
    unnamed x1 -> x0, blocking collectives: 10.9 us -> none
    reshape x7 -> x0, local copies, waits for them, and re-layouts: 10.1 us -> none  [the longest x1 6.48 us: on_device(): tile_blocks = a_vals.reshape(block_width, slot_total, block_width)]
    gather x3 -> x0, local copies, waits for them, and re-layouts: 9.04 us -> none  [the longest x1 4.11 us: on_device(): right = jnp.take(col_blocks, slot_cols, axis=1)]
    all_to_all x2 -> x0, starting transfers between devices: 8.8 us -> none  [the longest x1 5.51 us: on_device(): lax.all_to_all(send_vals, 'col', split_axis=0, concat_axis=0, tiled=True)]
    all_to_all x2 -> x0, waiting for transfers between devices: 6.75 us -> none  [the longest x1 6.75 us: on_device(): lax.all_to_all(send_vals, 'col', split_axis=0, concat_axis=0, tiled=True)]
  transfers between devices with their start and end apart: 3 -> 0, of which waited for: 2 -> 0; matrix products, arithmetic and copies ran while one was open for 35% -> 0% of each run, Pallas kernels for 0% -> 0%
where the time goes in v1:
time: 47.8 us; the launch traced here: 47.5 us
  Pallas kernels  35.6 us (74%)
  local copies, waits for them, and re-layouts  5.46 us (11%)
  other arithmetic  3.4 us (7%)
  between operations  2.96 us (6%)
    pallas_call x1, Pallas kernels, on_device(): pl.pallas_call(functools.partial(kernel, n_row, n_col), out_shape=jax.Sha...  35.6 us
    unnamed x5, local copies, waits for them, and re-layouts  3.07 us
    or x2, other arithmetic, on_device(): word = (key << sb | ids) << cb | a_cols[0]  1.41 us
    slice x1, local copies, waits for them, and re-layouts, on_device(): a_rows[0, 0] // dev_rows  1.16 us
    slice x1, local copies, waits for them, and re-layouts, on_device(): c_slot[0, 0]  1.16 us

profile of v1, /device:TPU:0, one launch (start us, length us, event | category | flops | bytes accessed | tf_op | source)
XLA Modules:
  0.0 47.5 jit_solution(3170376053679883858)
XLA Ops:
  0.7 1.2 %slice.15 = s32[1,1]{1,0:T(1,128)} slice(s32[1,256]{1,0:T(1,128)} %param.9), slice={[0:1], [0:1]} | slice | bytes 8 | tf_op jit(solution)/shard_map/slice | solution.py:245
  4.1 1.2 %slice.16 = s32[1,1]{1,0:T(1,128)} slice(s32[1,256]{1,0:T(1,128)} %param.12), slice={[0:1], [0:1]} | slice | bytes 8 | tf_op jit(solution)/shard_map/slice | solution.py:245
  5.2 0.6 %add_bitcast_fusion.k0_ref = s32[1,3]{1,0:T(1,128)S(1)} fusion(s32[1]{0:T(128)} %bitcast.12, s32[1]{0:T(128)} %bitcast.11, s32[1]{0:T(128)} %bitcast.10), kind=kLoop, calls=%fused_computation.20 | loop fusion | flops 6 | bytes 24 | tf_op jit(solution)/shard_map/broadcast_in_dim | solution.py:245
  5.9 0.7 %convert_element_type.12 = f32[8]{0:T(128)S(1)} convert(s32[8]{0:T(128)} %param.13) | non-fusion elementwise | flops 8 | bytes 64 | tf_op jit(solution)/shard_map/convert_element_type | solution.py:246
  6.5 0.7 %fusion.4 = s32[256]{0:T(256)S(1)} fusion(s32[256]{0:T(256)} %bitcast.23, s32[256]{0:T(256)} %bitcast.24, s32[]{:T(128)} %bitcast.18), kind=kLoop, calls=%fused_computation.14 | loop fusion | flops 1536 | bytes 3076 | tf_op jit(solution)/shard_map/or | solution.py:233
  7.2 0.7 %shift-left_or_fusion = (s32[1,256]{1,0:T(1,128)S(1)}, s32[1,256]{1,0:T(1,128)S(1)}) fusion(s32[1,256]{1,0:T(1,128)} %param.10, s32[1,256]{1,0:T(1,128)} %param.9, s32[]{:T(128)} %bitcast.17), kind=kLoop, calls=%fused_computation.19 | loop fusion | flops 1536 | bytes 4100 | tf_op jit(solution)/shard_map/or | solution.py:233
  7.9 0.2 convert_reduce_fusion
  8.1 0.1 select_reduce_fusion
  8.2 0.1 convert_reduce_fusion.1
  8.4 0.1 fusion
  8.5 0.1 slice_compare_fusion
  8.6 0.1 add_convert_fusion
  8.7 0.1 broadcast_in_dim.43.ag_ref
  8.7 0.0 copy-start
  8.7 1.6 %copy-done = bf16[64,16384]{1,0:T(8,128)(2,1)S(1)} copy-done((bf16[64,16384]{1,0:T(8,128)(2,1)S(1)}, bf16[64,16384]{1,0:T(8,128)(2,1)}, u32[]{:S(2)}) %copy-start) | copy-done | bytes 2097176
  10.3 0.0 copy-start.1
  10.3 0.8 %copy-done.1 = bf16[64,512]{1,0:T(8,128)(2,1)S(1)} copy-done((bf16[64,512]{1,0:T(8,128)(2,1)S(1)}, bf16[64,512]{1,0:T(8,128)(2,1)}, u32[]{:S(2)}) %copy-start.1) | copy-done | bytes 65560
  11.2 35.6 %shard_map.73 = f32[192,128]{1,0:T(8,128)S(1)} custom-call(s32[3,256]{1,0:T(4,128)S(1)} %pad_add_fusion.pk_ref, s32[1,64]{1,0:T(1,128)S(1)} %select_bitcast_fusion.idx_ref, s32[1,3]{1,0:T(1,128)S(1)} %add_bitcast_fusion.k0_ref, bf16[64,16384]{1,0:T(8,128)(2,1)S(1)} %copy-done, bf16[64,512]{1,0:T(8,128)(2,1)S(1)} %copy-done.1, ...), custom_call_target="tpu_custom_call" | custom-call | tf_op jit(solution)/shard_map/pallas_call | solution.py:251
  46.8 0.6 %copy.10 = f32[1,24576]{1,0:T(1,128)} copy(f32[1,24576]{1,0:T(1,128)S(1)} %bitcast.19) | data formatting | bytes 196608
  (3 shorter events, 0.0 us)
Async XLA Ops:
  8.7 1.6 %copy-start = (bf16[64,16384]{1,0:T(8,128)(2,1)S(1)}, bf16[64,16384]{1,0:T(8,128)(2,1)}, u32[]{:S(2)}) copy-start(bf16[64,16384]{1,0:T(8,128)(2,1)} %a_hbm.1) | copy-start | bytes 6291460
  10.3 0.8 %copy-start.1 = (bf16[64,512]{1,0:T(8,128)(2,1)S(1)}, bf16[64,512]{1,0:T(8,128)(2,1)}, u32[]{:S(2)}) copy-start(bf16[64,512]{1,0:T(8,128)(2,1)} %p_ref.1) | copy-start | bytes 196612

commit v2 on v1

--- a/solution.py
+++ b/solution.py
@@ -16,13 +16,48 @@
 BF16 = jnp.bfloat16
 
 
+def within(at, size):
+    return jnp.minimum(jnp.maximum(at, 0), size - 1)
+
+
+def make_plan(rows_group, cols_group, dev_rows, small, count_v, plan_v):
+    slots, width = small.shape[2], plan_v.shape[1]
+    cb, sb, db = (n.bit_length() - 1 for n in (cols_group, slots, dev_rows))
+    rows, cols = small[0], small[1]
+    lane = lax.broadcasted_iota(jnp.int32, (1, slots), 1)
+    key = jnp.where(lane < count_v[...], rows, rows_group)
+    across = jnp.broadcast_to(((((key << sb) | lane) << cb) | cols), (slots, slots))
+    side = lax.broadcasted_iota(jnp.int32, (slots, slots), 0)
+    place = lax.broadcasted_iota(jnp.int32, (slots, slots), 1)
+    down = jnp.sum(jnp.where(side == place, across, 0), axis=1, keepdims=True)
+    rank = jnp.sum(jnp.where(across < down, 1, 0), axis=1, keepdims=True)
+    word = jnp.sum(jnp.where(rank == place, down, 0), axis=0, keepdims=True)
+    slot = (word >> cb) & (slots - 1)
+    top = word >> (cb + sb)
+    same = (top == pltpu.roll(top, 1, 1)) & (lane > 0)
+    target = lax.broadcasted_iota(jnp.int32, (slots, width), 1)
+    tops = down >> (cb + sb)
+    upto = jnp.sum(jnp.where(tops <= target, 1, 0), axis=0, keepdims=True)
+    before = jnp.sum(jnp.where(tops < target, 1, 0), axis=0, keepdims=True)
+    last = jnp.where(upto > before, upto - 1, slots)
+    plan_v[...] = jnp.zeros_like(plan_v)
+    plan_v[0:1, :slots] = slot >> 1
+    plan_v[1:2, :slots] = 2 * (word & (cols_group - 1)) + (slot & 1)
+    plan_v[2:3, :slots] = same.astype(jnp.int32)
+    plan_v[3:4, :] = last
+    plan_v[4:5, :slots] = rows >> db
+    plan_v[5:6, :slots] = rows & (dev_rows - 1)
+    plan_v[6:7, :slots] = small[2]
+
+
 def kernel(
-    n_row, n_col, pk_ref, idx_ref, k0_ref, a_hbm, p_ref, ag_ref, out_ref,
-    a_v, pan, agp, colp, pz, ps, q_ref, snd, rcv,
+    n_row, n_col, a_hbm, p_hbm, rows_hbm, cols_hbm, count_hbm, kslot_hbm, agg_hbm, out_ref,
+    small, count_v, agg_v, plan_v, plan_s, ag_ref, in_sem, plan_sem, a_v, pan, agp, colp, pz, ps, q_ref, snd, rcv,
     a_sem, p_send, p_recv, g_send, g_recv, c_send, c_recv, x_send, x_recv,
 ):
-    bw = p_ref.shape[0]
+    bw = p_hbm.shape[0]
     dev_rows = ag_ref.shape[0]
+    rows_group = n_col * dev_rows
     slots = ps.shape[0] - 1
     ratio = n_col // n_row
     per = n_col // ratio
@@ -34,6 +69,23 @@
     is_root = row == me // ratio
     part = lax.rem(me, ratio)
 
+    p_ref = pan.at[me]
+    loads = [
+        pltpu.make_async_copy(src, dst, in_sem.at[i])
+        for i, (src, dst) in enumerate(
+            [
+                (p_hbm, p_ref),
+                (rows_hbm, small.at[0]),
+                (cols_hbm, small.at[1]),
+                (kslot_hbm, small.at[2]),
+                (count_hbm, count_v),
+                (agg_hbm, agg_v),
+            ]
+        )
+    ]
+    for c in loads:
+        c.start()
+
     @pl.loop(0, slots // 2)
     def _(i):
         lanes = pl.ds(pl.multiple_of(i * (2 * bw), 2 * bw), 2 * bw)
@@ -49,8 +101,15 @@
         pl.semaphore_signal(
             barrier, inc=1, device_id=(lax.rem(row + d, n_row), me), device_id_type=MESH
         )
-    pan[me] = p_ref[...]
-    agp[me] = ag_ref[...]
+    for c in loads:
+        c.wait()
+    square = (dev_rows, dev_rows)
+    eye = lax.broadcasted_iota(jnp.int32, square, 0) == lax.broadcasted_iota(jnp.int32, square, 1)
+    mine = jnp.where(eye, jnp.broadcast_to(agg_v[...].astype(F32), square), 0.0)
+    mine = jnp.broadcast_to(jnp.sum(mine, axis=1, keepdims=True), ag_ref.shape)
+    ag_ref[...] = mine
+    agp[me] = mine
+    make_plan(rows_group, n_col // (n_col // n_row) * dev_rows, dev_rows, small, count_v, plan_v)
     pl.semaphore_wait(barrier, n_col + n_row - 2)
 
     def remote(src, dst, s, r, dev):
@@ -83,6 +142,8 @@
             for c in panel_copies(q, src):
                 c.start()
 
+    plan_copy = pltpu.make_async_copy(plan_v, plan_s, plan_sem)
+    plan_copy.start()
     hand_on(me, p_ref)
     marks = [
         remote(ag_ref, agp.at[me], g_send.at[d - 1], g_recv.at[me], (row, col_of(d)))
@@ -132,12 +193,14 @@
             pz[2 * (m * dev_rows + b) + 1, bw:2 * bw, :] = block
     pltpu.make_async_copy(a_v, a_v, a_sem).wait()
 
+    plan_copy.wait()
+
     def steps(it, acc):
         for u in range(UNROLL):
             at = it * UNROLL + u
-            left = a_v[pk_ref[0, at]]
-            right = pz[pk_ref[1, at]]
-            keep = pk_ref[2, at].astype(F32)
+            left = a_v[within(plan_s[0, at], slots // 2)]
+            right = pz[within(plan_s[1, at], pz.shape[0])]
+            keep = plan_s[2, at].astype(F32)
             prod = jnp.dot(left, right, preferred_element_type=F32)
             acc = acc * keep + prod
             ps[at] = acc.astype(BF16)
@@ -169,7 +232,7 @@
                     )
                 )
             right = jnp.concatenate(
-                [ps[idx_ref[0, c * dev_rows + 4 * h + e]] for e in range(4)], axis=0
+                [ps[within(plan_s[3, c * dev_rows + 4 * h + e], slots + 1)] for e in range(4)], axis=0
             )
             total += jnp.dot(
                 jnp.concatenate(wide, axis=1), right, preferred_element_type=F32
@@ -193,9 +256,9 @@
         c.start()
     rcv[me] = snd[me]
 
-    there = lax.broadcasted_iota(jnp.int32, (dev_rows, 2 * bw), 0) == k0_ref[0, 1]
-    spot = jnp.sum(jnp.where(there, agp[k0_ref[0, 0]], 0.0), axis=0, keepdims=True)
-    spot = spot.astype(jnp.int32) * KC + k0_ref[0, 2]
+    there = lax.broadcasted_iota(jnp.int32, (dev_rows, 2 * bw), 0) == plan_s[5, 0]
+    spot = jnp.sum(jnp.where(there, agp[within(plan_s[4, 0], n_col)], 0.0), axis=0, keepdims=True)
+    spot = spot.astype(jnp.int32) * KC + plan_s[6, 0]
     for d in range(1, n_col):
         q = col_of(d)
         remote(snd.at[0], rcv.at[q], x_send.at[0], x_recv.at[q], (row, partner)).wait_recv()
@@ -225,35 +288,25 @@
     ratio = n_col // n_row
     cols_group = rows_group // ratio
     per = n_col // ratio
-    assert rows_group // AGG == n_col and n_col & (n_col - 1) == 0 and n_col >= KC
-    cb = (cols_group - 1).bit_length()
-    sb = (slots - 1).bit_length()
-    ids = jnp.arange(slots, dtype=jnp.int32)
-    key = jnp.where(ids < a_count[0, 0], a_rows[0], rows_group)
-    word = (((key << sb) | ids) << cb) | a_cols[0]
-    rank = jnp.sum((word[None, :] < word[:, None]).astype(jnp.int32), axis=1)
-    packed = jnp.sum(jnp.where(rank[None, :] == ids[:, None], word[None, :], 0), axis=1)
-    tops = packed >> (cb + sb)
-    keep = jnp.concatenate([jnp.zeros((1,), jnp.int32), (tops[1:] == tops[:-1]).astype(jnp.int32)])
-    slot = (packed >> cb) & ((1 << sb) - 1)
-    col = packed & ((1 << cb) - 1)
-    plan = jnp.stack([slot >> 1, 2 * col + (slot & 1), keep])
-    rows = jnp.arange(rows_group, dtype=jnp.int32)
-    upto = jnp.sum((key[None, :] <= rows[:, None]).astype(jnp.int32), axis=1)
-    seen = jnp.any(key[None, :] == rows[:, None], axis=1)
-    last = jnp.where(seen, upto - 1, slots)
-    lead = jnp.stack([a_rows[0, 0] // dev_rows, a_rows[0, 0] % dev_rows, c_slot[0, 0]])[None]
-    marks = jnp.broadcast_to(agg.astype(F32)[:, None], (dev_rows, 2 * bw))
-    smem = pl.BlockSpec(memory_space=pltpu.SMEM)
+    assert rows_group // AGG == n_col and n_col >= KC
+    assert all(n & (n - 1) == 0 for n in (n_col, slots, cols_group, dev_rows))
+    keep = pl.BlockSpec(memory_space=pltpu.HBM)
     vmem = pl.BlockSpec(memory_space=pltpu.VMEM)
     dma = pltpu.SemaphoreType.DMA
     owners = per * dev_rows // AGG
     out = pl.pallas_call(
         functools.partial(kernel, n_row, n_col),
         out_shape=jax.ShapeDtypeStruct((KC * bw // 2, 2 * bw), F32),
-        in_specs=[smem, smem, smem, pl.BlockSpec(memory_space=pl.ANY), vmem, vmem],
+        in_specs=[keep] * 7,
         out_specs=vmem,
         scratch_shapes=[
+            pltpu.VMEM((3, 1, slots), jnp.int32),
+            pltpu.VMEM((1, 1), jnp.int32),
+            pltpu.VMEM((1, dev_rows), jnp.int32),
+            pltpu.VMEM((8, max(slots, rows_group)), jnp.int32),
+            pltpu.SMEM((8, max(slots, rows_group)), jnp.int32),
+            pltpu.VMEM((dev_rows, 2 * bw), F32),
+            dma((6,)), dma,
             pltpu.VMEM((slots // 2, bw, 2 * bw), BF16),
             pltpu.VMEM((n_col, bw, dev_rows * bw), BF16),
             pltpu.VMEM((n_col, dev_rows, 2 * bw), F32),
@@ -270,9 +323,9 @@
             dma((n_col,)), dma((n_col,)),
         ],
         compiler_params=pltpu.CompilerParams(
-            collective_id=0, has_side_effects=True, vmem_limit_bytes=48 << 20
+            collective_id=0, has_side_effects=True, vmem_limit_bytes=67043328
         ),
-    )(plan, last.reshape(1, rows_group), lead, a_vals, p_vals, marks)
+    )(a_vals, p_vals, a_rows, a_cols, a_count, c_slot, agg.reshape(1, dev_rows))
     return out.reshape(1, KC * bw * bw)
 
 

time: 47.8 us -> 37.8 us (0.79)
  local copies, waits for them, and re-layouts: 5.46 us -> 1.54 us
  other arithmetic: 3.4 us -> 0 us
  between operations: 2.96 us -> 0.66 us
    slice x2 -> x0, local copies, waits for them, and re-layouts: 2.32 us -> none  [the longest x1 1.16 us: on_device(): a_rows[0, 0] // dev_rows]
    unnamed x5 -> x1, local copies, waits for them, and re-layouts: 3.07 us -> 1.54 us
    or x2 -> x0, other arithmetic: 1.41 us -> none  [on_device(): word = (key << sb | ids) << cb | a_cols[0]]
    convert_element_type x1 -> x0, other arithmetic: 0.66 us -> none  [on_device(): marks = jnp.broadcast_to(agg.astype(F32)[:, None], (dev_rows, 2 * bw))]
    broadcast_in_dim x1 -> x0, other arithmetic: 0.63 us -> none  [on_device(): jnp.stack([a_rows[0, 0] // dev_rows, a_rows[0, 0] % dev_rows, c_slot[0, 0]])]
where the time goes in v2:
time: 37.8 us; the launch traced here: 37.7 us
  Pallas kernels  35.5 us (94%)
  local copies, waits for them, and re-layouts  1.54 us (4%)
  between operations  0.66 us (2%)
    pallas_call x1, Pallas kernels, on_device(): pl.pallas_call(functools.partial(kernel, n_row, n_col), out_shape=jax.Sha...  35.5 us
    unnamed x1, local copies, waits for them, and re-layouts  1.54 us

profile of v2, /device:TPU:0, one launch (start us, length us, event | category | flops | bytes accessed | tf_op | source)
XLA Modules:
  0.0 37.7 jit_solution(17357388503483170015)
XLA Ops:
  0.7 35.5 %shard_map.73 = f32[192,128]{1,0:T(8,128)} custom-call(bf16[64,16384]{1,0:T(8,128)(2,1)} %a_hbm.1, bf16[64,512]{1,0:T(8,128)(2,1)} %p_hbm.1, s32[1,256]{1,0:T(1,128)} %rows_hbm.1, s32[1,256]{1,0:T(1,128)} %cols_hbm.1, s32[1,1]{1,0:T(1,128)S(6)} %copy.9.count_hbm, s32[1,256]{1,0:T(1,128)} %kslot_hbm.1, s32[1,8]{1,0:T(1,128)} %bitcast.3), custom_call_target="tpu_custom_call" | custom-call | tf_op jit(solution)/shard_map/pallas_call | solution.py:297
  36.1 1.5 %copy.10 = f32[1,24576]{1,0:T(1,128)} copy(f32[1,24576]{1,0:T(1,128)} %bitcast.2) | data formatting | bytes 196608

commit v3 on v2

--- a/solution.py
+++ b/solution.py
@@ -10,7 +10,7 @@
 AGG = 8
 KC = 6
 LO = 2
-UNROLL = 8
+UNROLL = 32
 MESH = pl.DeviceIdType.MESH
 F32 = jnp.float32
 BF16 = jnp.bfloat16
@@ -41,9 +41,8 @@
     before = jnp.sum(jnp.where(tops < target, 1, 0), axis=0, keepdims=True)
     last = jnp.where(upto > before, upto - 1, slots)
     plan_v[...] = jnp.zeros_like(plan_v)
-    plan_v[0:1, :slots] = slot >> 1
-    plan_v[1:2, :slots] = 2 * (word & (cols_group - 1)) + (slot & 1)
-    plan_v[2:3, :slots] = same.astype(jnp.int32)
+    right = 2 * (word & (cols_group - 1)) + (slot & 1)
+    plan_v[0:1, :slots] = (slot >> 1) | (same.astype(jnp.int32) << 15) | (right << 16)
     plan_v[3:4, :] = last
     plan_v[4:5, :slots] = rows >> db
     plan_v[5:6, :slots] = rows & (dev_rows - 1)
@@ -69,6 +68,16 @@
     is_root = row == me // ratio
     part = lax.rem(me, ratio)
 
+    def col_of(d):
+        return lax.rem(me + d, n_col)
+
+    barrier = pltpu.get_barrier_semaphore()
+    for d in range(1, n_col):
+        pl.semaphore_signal(barrier, inc=1, device_id=(row, col_of(d)), device_id_type=MESH)
+    for d in range(1, n_row):
+        pl.semaphore_signal(
+            barrier, inc=1, device_id=(lax.rem(row + d, n_row), me), device_id_type=MESH
+        )
     p_ref = pan.at[me]
     loads = [
         pltpu.make_async_copy(src, dst, in_sem.at[i])
@@ -86,21 +95,6 @@
     for c in loads:
         c.start()
 
-    @pl.loop(0, slots // 2)
-    def _(i):
-        lanes = pl.ds(pl.multiple_of(i * (2 * bw), 2 * bw), 2 * bw)
-        pltpu.make_async_copy(a_hbm.at[:, lanes], a_v.at[i], a_sem).start()
-
-    def col_of(d):
-        return lax.rem(me + d, n_col)
-
-    barrier = pltpu.get_barrier_semaphore()
-    for d in range(1, n_col):
-        pl.semaphore_signal(barrier, inc=1, device_id=(row, col_of(d)), device_id_type=MESH)
-    for d in range(1, n_row):
-        pl.semaphore_signal(
-            barrier, inc=1, device_id=(lax.rem(row + d, n_row), me), device_id_type=MESH
-        )
     for c in loads:
         c.wait()
     square = (dev_rows, dev_rows)
@@ -152,6 +146,13 @@
     for c in marks:
         c.start()
 
+    @pl.loop(0, slots // 16)
+    def _(g):
+        for u in range(8):
+            i = g * 8 + u
+            lanes = pl.ds(pl.multiple_of(i * (2 * bw), 2 * bw), 2 * bw)
+            pltpu.make_async_copy(a_hbm.at[:, lanes], a_v.at[i], a_sem).start()
+
     pz[...] = jnp.zeros_like(pz)
     ps[slots] = jnp.zeros((bw, bw), BF16)
     q_ref[...] = jnp.zeros_like(q_ref)
@@ -198,9 +199,10 @@
     def steps(it, acc):
         for u in range(UNROLL):
             at = it * UNROLL + u
-            left = a_v[within(plan_s[0, at], slots // 2)]
-            right = pz[within(plan_s[1, at], pz.shape[0])]
-            keep = plan_s[2, at].astype(F32)
+            word = plan_s[0, at]
+            left = a_v[word & (slots // 2 - 1)]
+            right = pz[(word >> 16) & (pz.shape[0] - 1)]
+            keep = ((word >> 15) & 1).astype(F32)
             prod = jnp.dot(left, right, preferred_element_type=F32)
             acc = acc * keep + prod
             ps[at] = acc.astype(BF16)
@@ -214,7 +216,7 @@
 
     lane = lax.broadcasted_iota(jnp.int32, (1, 2 * bw), 1)
 
-    def fold(c, carry):
+    def fold(c):
         group = c // per
         base = (group * owners).astype(F32)
         total = jnp.zeros((owners * bw, bw), F32)
@@ -237,10 +239,13 @@
             total += jnp.dot(
                 jnp.concatenate(wide, axis=1), right, preferred_element_type=F32
             )
-        q_ref[group] += total
+        return total
+
+    def fold_two(i, carry):
+        q_ref[2 * i // per] += fold(2 * i) + fold(2 * i + 1)
         return carry
 
-    lax.fori_loop(0, n_col, fold, 0)
+    lax.fori_loop(0, n_col // 2, fold_two, 0)
 
     half = bw // 2
     for o in range(n_col):
@@ -269,7 +274,7 @@
         for k in range(KC):
             sums[k] += jnp.where(where == k, value, 0.0)
     for k in range(KC):
-        out_ref[k * half:(k + 1) * half, :] = sums[k]
+        out_ref[k * half:(k + 1) * half, :] = sums[k].astype(BF16)
 
     for c in own + passed + marks + terms:
         c.wait_send()
@@ -296,7 +301,7 @@
     owners = per * dev_rows // AGG
     out = pl.pallas_call(
         functools.partial(kernel, n_row, n_col),
-        out_shape=jax.ShapeDtypeStruct((KC * bw // 2, 2 * bw), F32),
+        out_shape=jax.ShapeDtypeStruct((KC * bw // 2, 2 * bw), BF16),
         in_specs=[keep] * 7,
         out_specs=vmem,
         scratch_shapes=[
@@ -326,7 +331,7 @@
             collective_id=0, has_side_effects=True, vmem_limit_bytes=67043328
         ),
     )(a_vals, p_vals, a_rows, a_cols, a_count, c_slot, agg.reshape(1, dev_rows))
-    return out.reshape(1, KC * bw * bw)
+    return out.astype(F32).reshape(1, KC * bw * bw)
 
 
 def solution(mesh):

time: 37.8 us -> 32.4 us (0.86)
  Pallas kernels: 35.5 us -> 30 us
  local copies, waits for them, and re-layouts: 1.54 us -> 0 us
  other arithmetic: 0 us -> 1.45 us
    pallas_call x1, Pallas kernels: 35.5 us -> 30 us  [on_device(): pl.pallas_call(functools.partial(kernel, n_row, n_col), out_shape=jax.Sha...]
    unnamed x1 -> x0, local copies, waits for them, and re-layouts: 1.54 us -> none
    reshape x0 -> x1, other arithmetic: none -> 1.45 us  [on_device(): return out.astype(F32).reshape(1, KC * bw * bw)]
where the time goes in v3:
time: 32.4 us; the launch traced here: 32.1 us
  Pallas kernels  30 us (93%)
  other arithmetic  1.45 us (4%)
  between operations  0.66 us (2%)
    pallas_call x1, Pallas kernels, on_device(): pl.pallas_call(functools.partial(kernel, n_row, n_col), out_shape=jax.Sha...  30 us
    reshape x1, other arithmetic, on_device(): return out.astype(F32).reshape(1, KC * bw * bw)  1.45 us

profile of v3, /device:TPU:0, one launch (start us, length us, event | category | flops | bytes accessed | tf_op | source)
XLA Modules:
  0.0 32.1 jit_solution(8521599446435457542)
XLA Ops:
  0.7 30.0 %shard_map.73 = bf16[192,128]{1,0:T(8,128)(2,1)} custom-call(bf16[64,16384]{1,0:T(8,128)(2,1)} %a_hbm.1, bf16[64,512]{1,0:T(8,128)(2,1)} %p_hbm.1, s32[1,256]{1,0:T(1,128)} %rows_hbm.1, s32[1,256]{1,0:T(1,128)} %cols_hbm.1, s32[1,1]{1,0:T(1,128)S(6)} %copy.8.count_hbm, s32[1,256]{1,0:T(1,128)} %kslot_hbm.1, s32[1,8]{1,0:T(1,128)} %bitcast.2), custom_call_target="tpu_custom_call" | custom-call | tf_op jit(solution)/shard_map/pallas_call | solution.py:302
  30.7 1.4 %reshape.12 = f32[192,128]{1,0:T(8,128)} convert(bf16[192,128]{1,0:T(8,128)(2,1)} %shard_map.73) | non-fusion elementwise | flops 24576 | bytes 147456 | tf_op jit(solution)/shard_map/reshape | solution.py:334

commit v4 on v3

--- a/solution.py
+++ b/solution.py
@@ -245,20 +245,25 @@
         q_ref[2 * i // per] += fold(2 * i) + fold(2 * i + 1)
         return carry
 
-    lax.fori_loop(0, n_col // 2, fold_two, 0)
-
     half = bw // 2
-    for o in range(n_col):
-        g, w = o // owners, o % owners
-        even = q_ref[g, pl.ds(w * bw, half, stride=2), :]
-        odd = q_ref[g, pl.ds(w * bw + 1, half, stride=2), :]
-        snd[o] = jnp.concatenate([even, odd], axis=1).astype(BF16)
-    terms = []
-    for d in range(1, n_col):
-        to = col_of(d)
-        terms.append(remote(snd.at[to], rcv.at[me], x_send.at[d - 1], x_recv.at[me], (row, to)))
-    for c in terms:
-        c.start()
+
+    def term(o):
+        return remote(snd.at[o], rcv.at[me], x_send.at[o], x_recv.at[me], (row, o))
+
+    for g in range(ratio):
+        lax.fori_loop(g * per // 2, (g + 1) * per // 2, fold_two, 0)
+        for w in range(owners):
+            o = g * owners + w
+            even = q_ref[g, pl.ds(w * bw, half, stride=2), :]
+            odd = q_ref[g, pl.ds(w * bw + 1, half, stride=2), :]
+            snd[o] = jnp.concatenate([even, odd], axis=1).astype(BF16)
+        for w in range(owners):
+            o = g * owners + w
+
+            @pl.when(me != o)
+            def _():
+                term(o).start()
+
     rcv[me] = snd[me]
 
     there = lax.broadcasted_iota(jnp.int32, (dev_rows, 2 * bw), 0) == plan_s[5, 0]
@@ -276,8 +281,13 @@
     for k in range(KC):
         out_ref[k * half:(k + 1) * half, :] = sums[k].astype(BF16)
 
-    for c in own + passed + marks + terms:
+    for c in own + passed + marks:
         c.wait_send()
+    for o in range(n_col):
+        @pl.when(me != o)
+        def _():
+            term(o).wait_send()
+
     for m in range(per):
         @pl.when(is_root)
         def _():

time: 32.4 us -> 31.4 us (0.969)
  Pallas kernels: 30 us -> 29 us
    pallas_call x1, Pallas kernels: 30 us -> 29 us  [on_device(): pl.pallas_call(functools.partial(kernel, n_row, n_col), out_shape=jax.Sha...]
where the time goes in v4:
time: 31.4 us; the launch traced here: 31.2 us
  Pallas kernels  29 us (92%)
  other arithmetic  1.45 us (5%)
  between operations  0.66 us (2%)
    pallas_call x1, Pallas kernels, on_device(): pl.pallas_call(functools.partial(kernel, n_row, n_col), out_shape=jax.Sha...  29 us
    reshape x1, other arithmetic, on_device(): return out.astype(F32).reshape(1, KC * bw * bw)  1.45 us

profile of v4, /device:TPU:0, one launch (start us, length us, event | category | flops | bytes accessed | tf_op | source)
XLA Modules:
  0.0 31.2 jit_solution(6496667888612302217)
XLA Ops:
  0.7 29.0 %shard_map.73 = bf16[192,128]{1,0:T(8,128)(2,1)} custom-call(bf16[64,16384]{1,0:T(8,128)(2,1)} %a_hbm.1, bf16[64,512]{1,0:T(8,128)(2,1)} %p_hbm.1, s32[1,256]{1,0:T(1,128)} %rows_hbm.1, s32[1,256]{1,0:T(1,128)} %cols_hbm.1, s32[1,1]{1,0:T(1,128)S(6)} %copy.8.count_hbm, s32[1,256]{1,0:T(1,128)} %kslot_hbm.1, s32[1,8]{1,0:T(1,128)} %bitcast.2), custom_call_target="tpu_custom_call" | custom-call | tf_op jit(solution)/shard_map/pallas_call | solution.py:312
  29.7 1.4 %reshape.12 = f32[192,128]{1,0:T(8,128)} convert(bf16[192,128]{1,0:T(8,128)(2,1)} %shard_map.73) | non-fusion elementwise | flops 24576 | bytes 147456 | tf_op jit(solution)/shard_map/reshape | solution.py:344
